TPU v7x, 32 devices: a whole 2x2x4 slice. The times are simulated.
32 devices in a mesh: seq: 8 (over z, y), head: 4 (over x, core).
Axes of the slice: x: 2, y: 2, z: 4, core: 2. Of those that a mesh axis runs over, the one named last changes fastest.
Arguments:
- queries: bfloat16 [8, 1024, 128], P('head', 'seq')
- keys: bfloat16 [8, 1024, 128], P('head', 'seq')
- values: bfloat16 [8, 1024, 128], P('head', 'seq'), may hold values from -6 to 6
- grad_out: bfloat16 [8, 1024, 128], P('head', 'seq'), may hold values from -96 to 96
- rand_ids: int32 [8, 16, 3], P('head', 'seq'), may hold values from 0 to 15, as said below
- global_ids: int32 [2], replicated, may hold values from 0 to 15
Outputs:
- grad_queries: bfloat16 [8, 1024, 128], P('head', 'seq')
- grad_keys: bfloat16 [8, 1024, 128], P('head', 'seq')
- grad_values: bfloat16 [8, 1024, 128], P('head', 'seq')
Inputs may be any that keep to these rules, and one draw needn't show every extreme that they name: `rand_ids`: for each head and slot j there is one number M, 0 <= M < 8, such that every query block b names in slot j a block e * 2 + l with e = (b // 2) XOR M and 0 <= l < 2.
All inputs are finite; a program needn't handle non-finite values.
Results may differ from a plain program's by a relative error of at most 0.03.
Values may be sent and summed in bfloat16 or wider, within the bound.
No kernel may reach another device: no remote copies, remote signals or barrier semaphores. Data moves between devices by JAX's collectives and lax.ppermute only.
A program may use at most 64 MiB of HBM per device.

v0:
```python
import math
import jax
import jax.numpy as jnp
from jax import lax
from jax.sharding import PartitionSpec as P


def with_halo(value, sides, width):
    for axis, dim in sides:
        peers, length = (lax.axis_size(axis), value.shape[dim])
        up = [(i, (i + 1) % peers) for i in range(peers - 1)]
        down = [(j, i) for i, j in up]
        last = lax.slice_in_dim(value, length - width, length, axis=dim)
        initial = lax.slice_in_dim(value, 0, width, axis=dim)
        before = lax.ppermute(last, axis, up)
        after = lax.ppermute(initial, axis, down)
        value = jnp.concatenate([before, value, after], axis=dim)
    return value


def swapped(value, axis, distance):
    mask = 2**distance
    pairs = [(source, source ^ mask) for source in range(lax.axis_size(axis))]
    return lax.ppermute(value, axis, pairs)


def section_list(section_count):
    return list(range(section_count))


def on_device(queries, keys, values, grad_out, rand_ids, global_ids):
    head_count, row_count, head_width = queries.shape
    block_count = rand_ids.shape[1]
    slot_count = rand_ids.shape[2]
    block_rows = row_count // block_count
    global_count = global_ids.shape[0]
    slot_total = 3 + global_count + slot_count
    device = lax.axis_index("seq")
    seq_count = lax.axis_size("seq")
    sections = section_list(seq_count.bit_length() - 1)
    score_scale = 1.0 / math.sqrt(head_width)
    key_vals = jnp.stack([keys, values])
    padded = with_halo(key_vals, (("seq", 2),), block_rows)
    padded_blocks = padded.reshape(2, head_count, block_count + 2, block_rows, head_width)
    window = jnp.stack(
        [
            padded_blocks[:, :, 0:block_count],
            padded_blocks[:, :, 1 : block_count + 1],
            padded_blocks[:, :, 2 : block_count + 2],
        ],
        3,
    )
    key_blocks = key_vals.reshape(2, head_count, block_count, block_rows, head_width)
    global_local = global_ids % block_count
    global_owner = global_ids // block_count
    owned = (global_owner == device).astype(jnp.float32)
    picked = jnp.take(key_blocks, global_local, axis=2).astype(jnp.float32)
    global_sum = lax.psum(picked * owned[None, None, :, None, None], "seq")
    global_kv = global_sum.astype(jnp.bfloat16)
    global_keys = jnp.broadcast_to(
        global_kv[:, :, None], (2, head_count, block_count, global_count, block_rows, head_width)
    )
    xor_masks = jnp.bitwise_xor(rand_ids[:, 0, :] // block_count, device)
    pieces = []
    for slot_index in range(slot_count):
        moving = key_vals
        for bit_index in sections:
            arrived = swapped(moving, "seq", bit_index)
            flag_now = jnp.right_shift(xor_masks[:, slot_index], bit_index) & 1 == 1
            moving = jnp.where(flag_now[None, :, None, None], arrived, moving)
        pieces.append(moving)
    routed = jnp.stack(pieces)
    routed_blocks = routed.reshape(slot_count, 2, head_count, block_count, block_rows, head_width)
    random_local = rand_ids % block_count
    local_onehot = (random_local[..., None] == jnp.arange(block_count, dtype=jnp.int32)).astype(
        jnp.bfloat16
    )
    random_keys = jnp.einsum(
        "hqjl,jchlbd->chqjbd", local_onehot, routed_blocks, preferred_element_type=jnp.float32
    ).astype(jnp.bfloat16)
    all_keys = jnp.concatenate([window, global_keys, random_keys], axis=3)
    key_list = all_keys[0].reshape(head_count, block_count, slot_total * block_rows, head_width)
    value_list = all_keys[1].reshape(head_count, block_count, slot_total * block_rows, head_width)
    block_range = jnp.arange(block_count, dtype=jnp.int32)
    left_valid = jnp.logical_not((block_range == 0) & (device == 0))
    right_valid = jnp.logical_not((block_range == block_count - 1) & (device == seq_count - 1))
    valid = jnp.concatenate(
        [
            left_valid[:, None],
            jnp.ones((block_count, 1), bool),
            right_valid[:, None],
            jnp.ones((block_count, global_count + slot_count), bool),
        ],
        1,
    )
    mask = jnp.repeat(valid, block_rows, axis=1)[None, :, None, :]
    query_blocks = queries.reshape(head_count, block_count, block_rows, head_width)
    grad_blocks = grad_out.reshape(head_count, block_count, block_rows, head_width)
    scores = (
        jnp.einsum("hnqd,hnkd->hnqk", query_blocks, key_list, preferred_element_type=jnp.float32)
        * score_scale
    )
    row_max = jnp.max(jnp.where(mask, scores, -1e30), -1)
    total = jnp.sum(jnp.where(mask, jnp.exp(scores - row_max[..., None]), 0.0), -1)
    log_total = row_max + jnp.log(total)
    probs = jnp.where(mask, jnp.exp(scores - log_total[..., None]), 0.0)
    probs_low = probs.astype(jnp.bfloat16)
    output = jnp.einsum(
        "hnqk,hnkd->hnqd", probs_low, value_list, preferred_element_type=jnp.float32
    )
    row_dot = jnp.sum(grad_blocks.astype(jnp.float32) * output, -1)
    grad_probs = jnp.einsum(
        "hnqd,hnkd->hnqk", grad_blocks, value_list, preferred_element_type=jnp.float32
    )
    scores_low = (probs * (grad_probs - row_dot[..., None])).astype(jnp.bfloat16)
    grad_query = score_scale * jnp.einsum(
        "hnqk,hnkd->hnqd", scores_low, key_list, preferred_element_type=jnp.float32
    )
    key_terms = score_scale * jnp.einsum(
        "hnqk,hnqd->hnkd", scores_low, query_blocks, preferred_element_type=jnp.float32
    )
    value_terms = jnp.einsum(
        "hnqk,hnqd->hnkd", probs_low, grad_blocks, preferred_element_type=jnp.float32
    )
    grads = jnp.stack([key_terms, value_terms]).reshape(
        2, head_count, block_count, slot_total, block_rows, head_width
    )
    no_pad = (0, 0)
    frame_sum = jnp.pad(grads[:, :, :, 0], (no_pad, no_pad, (0, 2), no_pad, no_pad))
    frame_sum = frame_sum + jnp.pad(grads[:, :, :, 1], (no_pad, no_pad, (1, 1), no_pad, no_pad))
    frame_sum = frame_sum + jnp.pad(grads[:, :, :, 2], (no_pad, no_pad, (2, 0), no_pad, no_pad))
    own_grads = frame_sum[:, :, 1 : block_count + 1]
    rim_parts = jnp.concatenate([frame_sum[:, :, 0], frame_sum[:, :, block_count + 1]], axis=2)
    rim_back = with_halo(rim_parts.astype(jnp.bfloat16), (("seq", 2),), block_rows).astype(
        rim_parts.dtype
    )
    own_grads = own_grads.at[:, :, 0].add(rim_back[:, :, 0:block_rows])
    own_grads = own_grads.at[:, :, block_count - 1].add(
        rim_back[:, :, 3 * block_rows : 4 * block_rows]
    )
    global_part = jnp.sum(grads[:, :, :, 3 : 3 + global_count], axis=2)
    global_total = lax.psum(global_part, "seq")
    global_onehot = (
        (global_local[:, None] == block_range[None, :]) & (global_owner == device)[:, None]
    ).astype(jnp.float32)
    own_grads = own_grads + jnp.einsum(
        "gn,chgbd->chnbd", global_onehot, global_total, precision=lax.Precision.HIGHEST
    )
    random_part = grads[:, :, :, 3 + global_count :]
    local_float = (random_local[..., None] == block_range).astype(jnp.float32)
    send_back = jnp.einsum(
        "hqjl,chqjbd->jchlbd", local_float, random_part, precision=lax.Precision.HIGHEST
    )
    send_back = send_back.astype(jnp.bfloat16).reshape(
        slot_count, 2, head_count, row_count, head_width
    )
    pieces = []
    for slot_index in range(slot_count):
        moving = send_back[slot_index]
        for bit_index in sections:
            arrived = swapped(moving, "seq", bit_index)
            flag_now = jnp.right_shift(xor_masks[:, slot_index], bit_index) & 1 == 1
            moving = jnp.where(flag_now[None, :, None, None], arrived, moving)
        pieces.append(moving)
    returned = jnp.stack(pieces)
    returned_sum = jnp.sum(returned.astype(jnp.float32), axis=0).reshape(
        2, head_count, block_count, block_rows, head_width
    )
    own_grads = own_grads + returned_sum
    grad_queries = grad_query.reshape(head_count, row_count, head_width).astype(jnp.bfloat16)
    grad_keys = own_grads[0].reshape(head_count, row_count, head_width).astype(jnp.bfloat16)
    grad_values = own_grads[1].reshape(head_count, row_count, head_width).astype(jnp.bfloat16)
    return (grad_queries, grad_keys, grad_values)


def solution(mesh):
    in_specs = (
        P("head", "seq", None),
        P("head", "seq", None),
        P("head", "seq", None),
        P("head", "seq", None),
        P("head", "seq", None),
        P(),
    )
    out_specs = (P("head", "seq", None), P("head", "seq", None), P("head", "seq", None))
    return jax.shard_map(
        on_device, mesh=mesh, in_specs=in_specs, out_specs=out_specs, check_vma=False
    )
```

profile of v0, /device:TPU:0, one launch (start us, length us, event | category | flops | bytes accessed | tf_op | source)
XLA Modules:
  0.0 174.2 jit_solution(11851105725441294419)
XLA Ops:
  7.2 0.9 fusion.24
  8.1 1.3 collective-permute-start.1
  9.4 5.5 %collective-permute-start = (bf16[2,2,64,128]{3,2,1,0:T(8,128)(2,1)S(1)}, bf16[2,2,64,128]{3,2,1,0:T(8,128)(2,1)S(1)}, u32[]{:S(2)}, u32[]{:S(2)}) collective-permute-start(bf16[2,2,64,128]{3,2,1,0:T(8,128)(2,1)S(1)} %get-tuple-element.60), channel_id=1, source_target_pairs={{0,4},{4,8},{8,12},{12,16},{16,20},{20,24},{24,28},{1,5},{5,9},{9,... | collective-permute-start | bytes 196616 | tf_op jit(solution)/shard_map/ppermute | solution.py:15
  15.0 3.0 %collective-permute-start.2 = (bf16[2,2,128,128]{3,2,1,0:T(8,128)(2,1)S(1)}, bf16[2,2,128,128]{3,2,1,0:T(8,128)(2,1)S(1)}, u32[]{:S(2)}, u32[]{:S(2)}) collective-permute-start(bf16[2,2,128,128]{3,2,1,0:T(8,128)(2,1)S(1)} %pad_maximum_fusion.7), channel_id=1, source_target_pairs={{0,4},{4,0},{8,12},{12,8},{16,20},{20,16},{24,28},{28,24},{1,5},{5... | collective-permute-start | bytes 393224 | tf_op jit(solution)/shard_map/ppermute | solution.py:24
  18.0 0.6 copy-done.5
  18.7 0.6 gather_fusion
  19.3 0.1 multiply_bitcast_fusion
  19.4 38.6 %all-reduce.7 = bf16[2,2,2,64,128]{4,3,1,0,2:T(8,128)(2,1)S(1)} all-reduce(f32[2,2,2,64,128]{4,3,1,0,2:T(8,128)S(1)} %multiply_bitcast_fusion), channel_id=1, replica_groups=mesh['seq'=8,'head'=4] {'seq'}, use_global_device_ids=true, to_apply=%region_0.1 | all-reduce | flops 65536 | bytes 393216 | tf_op jit(solution)/shard_map/psum | solution.py:58
  58.0 0.7 slice-done
  58.7 0.1 copy.53
  59.1 0.1 broadcast_in_dim.152
  59.2 0.3 compare_reduce_fusion.8
  59.6 0.1 fusion.23
  59.7 0.1 fusion.22
  59.9 0.1 fusion.21
  60.0 0.1 broadcast_select_fusion.11
  60.2 0.2 broadcast_dynamic-update-slice_fusion
  60.4 2.1 %collective-permute-start.5 = (bf16[2,2,128,128]{3,2,1,0:T(8,128)(2,1)S(1)}, bf16[2,2,128,128]{3,2,1,0:T(8,128)(2,1)S(1)}, u32[]{:S(2)}, u32[]{:S(2)}) collective-permute-start(bf16[2,2,128,128]{3,2,1,0:T(8,128)(2,1)S(1)} %get-tuple-element.54), channel_id=1, source_target_pairs={{0,8},{4,12},{8,0},{12,4},{16,24},{20,28},{24,16},{28,20},{1,9},{5... | collective-permute-start | bytes 393224 | tf_op jit(solution)/shard_map/ppermute | solution.py:24
  62.6 4.0 %collective-permute-done.7 = bf16[2,2,128,128]{3,2,1,0:T(8,128)(2,1)S(1)} collective-permute-done((bf16[2,2,128,128]{3,2,1,0:T(8,128)(2,1)S(1)}, bf16[2,2,128,128]{3,2,1,0:T(8,128)(2,1)S(1)}, u32[]{:S(2)}, u32[]{:S(2)}) %collective-permute-start.7) | collective-permute-done | bytes 131104 | tf_op jit(solution)/shard_map/ppermute | solution.py:24
  66.8 2.9 %collective-permute-done.5 = bf16[2,2,128,128]{3,2,1,0:T(8,128)(2,1)S(1)} collective-permute-done((bf16[2,2,128,128]{3,2,1,0:T(8,128)(2,1)S(1)}, bf16[2,2,128,128]{3,2,1,0:T(8,128)(2,1)S(1)}, u32[]{:S(2)}, u32[]{:S(2)}) %collective-permute-start.5) | collective-permute-done | bytes 131104 | tf_op jit(solution)/shard_map/ppermute | solution.py:24
  69.7 0.1 broadcast_select_fusion.8
  69.8 1.2 collective-permute-done.3
  71.2 1.7 %collective-permute-start.4 = (bf16[2,2,128,128]{3,2,1,0:T(8,128)(2,1)S(1)}, bf16[2,2,128,128]{3,2,1,0:T(8,128)(2,1)S(1)}, u32[]{:S(2)}, u32[]{:S(2)}) collective-permute-start(bf16[2,2,128,128]{3,2,1,0:T(8,128)(2,1)S(1)} %broadcast_select_fusion.13), channel_id=1, source_target_pairs={{0,16},{4,20},{8,24},{12,28},{16,0},{20,4},{24,8},{28,12},{1,17},{... | collective-permute-start | bytes 393224 | tf_op jit(solution)/shard_map/ppermute | solution.py:24
  72.9 3.4 %collective-permute-done.8 = bf16[2,2,128,128]{3,2,1,0:T(8,128)(2,1)S(1)} collective-permute-done((bf16[2,2,128,128]{3,2,1,0:T(8,128)(2,1)S(1)}, bf16[2,2,128,128]{3,2,1,0:T(8,128)(2,1)S(1)}, u32[]{:S(2)}, u32[]{:S(2)}) %collective-permute-start.8) | collective-permute-done | bytes 131104 | tf_op jit(solution)/shard_map/ppermute | solution.py:24
  76.3 0.1 copy.52
  76.5 1.7 collective-permute-done.6
  78.2 0.1 copy.51
  78.4 1.4 collective-permute-done.4
  79.9 0.1 copy.50
  80.0 0.8 fusion.4
  80.8 1.2 fusion.49
  82.0 0.4 select_reduce_fusion.1
  82.4 0.2 select_reduce_fusion
  82.7 0.6 copy-done.3
  83.3 0.5 fusion.28
  83.8 0.4 fusion.9
  84.2 0.3 fusion.1
  84.5 0.9 fusion.8
  85.4 0.3 convolution_multiply_fusion
  86.1 1.3 collective-permute-start.10
  87.4 4.7 %collective-permute-start.9 = (bf16[2,2,64,128]{3,2,1,0:T(8,128)(2,1)S(1)}, bf16[2,2,64,128]{3,2,1,0:T(8,128)(2,1)S(1)}, u32[]{:S(2)}, u32[]{:S(2)}) collective-permute-start(bf16[2,2,64,128]{3,2,1,0:T(8,128)(2,1)S(1)} %get-tuple-element.50), channel_id=1, source_target_pairs={{0,4},{4,8},{8,12},{12,16},{16,20},{20,24},{24,28},{1,5},{5,9},{9,... | collective-permute-start | bytes 196616 | tf_op jit(solution)/shard_map/ppermute | solution.py:15
  92.2 0.9 copy.63
  93.1 1.9 %fusion.2 = bf16[3,2,2,2,64,128]{5,3,4,1,2,0:T(2,128)(2,1)S(1)} fusion(f32[2,2,2,3,64,128]{5,4,3,2,1,0:T(8,128)S(1)} %pad_maximum_fusion, s32[2,2,3]{1,0,2:T(2,128)S(1)} %copy.53), kind=kOutput, calls=%fused_computation.8 | convolution fusion | flops 4915224 | bytes 1179696 | tf_op jit(solution)/shard_map/hqjl,chqjbd->jchlbd/dot_general | solution.py:151
  95.0 0.3 fusion.50
  95.5 2.1 %collective-permute-start.14 = (bf16[2,2,128,128]{3,2,1,0:T(8,128)(2,1)S(1)}, bf16[2,2,128,128]{3,2,1,0:T(8,128)(2,1)S(1)}, u32[]{:S(2)}, u32[]{:S(2)}) collective-permute-start(bf16[2,2,128,128]{3,2,1,0:T(8,128)(2,1)S(1)} %bitcast.125), channel_id=1, source_target_pairs={{0,4},{4,0},{8,12},{12,8},{16,20},{20,16},{24,28},{28,24},{1,5},{5... | collective-permute-start | bytes 393224 | tf_op jit(solution)/shard_map/ppermute | solution.py:24
  97.7 0.2 copy.62
  98.0 0.1 add.68
  98.1 2.6 %scatter-add.9 = f32[2,2,2,64,128]{4,2,3,1,0:T(2,128)S(1)} dynamic-update-slice(f32[2,2,2,64,128]{4,2,3,1,0:T(2,128)S(1)} %copy.62, f32[2,2,1,64,128]{4,2,3,1,0:T(1,128)S(1)} %add.68, s32[]{:T(128)} %constant.122.clone.1, s32[]{:T(128)} %constant.122.clone.1, s32[]{:T(128)} %constant.126.clone.1, s32[]{:T(128)} %constant.122.clone.1, s32[]{:T(128)} %constant.122.clone.1) | dynamic-update-slice | bytes 262148 | tf_op jit(solution)/shard_map/scatter-add | solution.py:138
  100.9 0.9 collective-permute-done.14
  101.9 1.2 collective-permute-start.15
  103.1 0.1 collective-permute-done.11
  103.3 0.8 collective-permute-start.12
  104.2 4.2 %collective-permute-done.18 = bf16[2,2,128,128]{3,2,1,0:T(8,128)(2,1)S(1)} collective-permute-done((bf16[2,2,128,128]{3,2,1,0:T(8,128)(2,1)S(1)}, bf16[2,2,128,128]{3,2,1,0:T(8,128)(2,1)S(1)}, u32[]{:S(2)}, u32[]{:S(2)}) %collective-permute-start.18) | collective-permute-done | bytes 131104 | tf_op jit(solution)/shard_map/ppermute | solution.py:24
  108.5 1.4 collective-permute-done.15
  110.0 1.5 collective-permute-start.16
  111.7 1.5 collective-permute-start.13
  113.2 4.5 %collective-permute-done.19 = bf16[2,2,128,128]{3,2,1,0:T(8,128)(2,1)S(1)} collective-permute-done((bf16[2,2,128,128]{3,2,1,0:T(8,128)(2,1)S(1)}, bf16[2,2,128,128]{3,2,1,0:T(8,128)(2,1)S(1)}, u32[]{:S(2)}, u32[]{:S(2)}) %collective-permute-start.19) | collective-permute-done | bytes 131104 | tf_op jit(solution)/shard_map/ppermute | solution.py:24
  117.7 1.6 collective-permute-done.16
  119.4 1.4 collective-permute-done.13
  121.0 43.2 %all-reduce.6.cloned.1.call-done = f32[2,2,2,64,128]{4,2,3,1,0:T(2,128)} async-done(((f32[2,2,2,64,128]{4,2,3,1,0:T(2,128)}), f32[2,2,2,64,128]{4,2,3,1,0:T(2,128)}) %all-reduce.6.cloned.1.call-update) | async-done | bytes 262160 | tf_op jit(solution)/shard_map/psum | solution.py:142
  164.1 1.8 %fusion.7 = bf16[2,2,2,64,128]{4,2,3,1,0:T(2,128)(2,1)S(1)} fusion(f32[2,2,2,64,128]{4,2,3,1,0:T(2,128)S(1)} %scatter-add.9, f32[2,2,2,64,128]{4,2,3,1,0:T(2,128)} %all-reduce.6.cloned.1.call-done, f32[2,2,2,64,128]{4,3,2,1,0:T(8,128)S(1)} %bitcast.136, pred[2]{0:T(512)(128)(4,1)S(1)} %get-tuple-element.63, s32[2]{0:T(128)S(1)} %get-tuple-element.39), kind=kOutput, calls=%fused_computation.14 | convolution fusion | flops 1769480 | bytes 917514 | tf_op jit(solution)/shard_map/gn,chgbd->chnbd/dot_general | solution.py:146
  165.9 0.1 fusion.52
  166.0 0.6 copy.69
  166.7 0.6 copy.70
  (74 shorter events, 2.8 us)
Async XLA Ops:
  7.2 74.9 %copy-start = (bf16[2,128,128]{2,1,0:T(8,128)(2,1)S(1)}, bf16[2,128,128]{2,1,0:T(8,128)(2,1)}, u32[]{:S(2)}) copy-start(bf16[2,128,128]{2,1,0:T(8,128)(2,1)} %param.10) | copy-start | bytes 196612
  7.2 157.0 %all-reduce.6.cloned.1.call-start = ((), (), s32[]{:S(2)}) async-start(), calls=%async_computation | async-start | bytes 524288 | tf_op jit(solution)/shard_map/psum | solution.py:142
  7.2 7.7 %copy-start.1 = (bf16[2,128,128]{2,1,0:T(8,128)(2,1)S(1)}, bf16[2,128,128]{2,1,0:T(8,128)(2,1)}, u32[]{:S(2)}) copy-start(bf16[2,128,128]{2,1,0:T(8,128)(2,1)} %param.11) | copy-start | bytes 196612
  7.2 7.7 %copy-start.2 = (bf16[2,128,128]{2,1,0:T(8,128)(2,1)S(1)}, bf16[2,128,128]{2,1,0:T(8,128)(2,1)}, u32[]{:S(2)}) copy-start(bf16[2,128,128]{2,1,0:T(8,128)(2,1)} %param.12) | copy-start | bytes 196612
  8.1 51.4 %collective-permute-start.1 = (bf16[2,2,64,128]{3,2,1,0:T(8,128)(2,1)S(1)}, bf16[2,2,64,128]{3,2,1,0:T(8,128)(2,1)S(1)}, u32[]{:S(2)}, u32[]{:S(2)}) collective-permute-start(bf16[2,2,64,128]{3,2,1,0:T(8,128)(2,1)S(1)} %get-tuple-element.61), channel_id=1, source_target_pairs={{4,0},{8,4},{12,8},{16,12},{20,16},{24,20},{28,24},{5,1},{9,5},{13... | collective-permute-start | bytes 196616 | tf_op jit(solution)/shard_map/ppermute | solution.py:16
  9.4 50.1 %collective-permute-start = (bf16[2,2,64,128]{3,2,1,0:T(8,128)(2,1)S(1)}, bf16[2,2,64,128]{3,2,1,0:T(8,128)(2,1)S(1)}, u32[]{:S(2)}, u32[]{:S(2)}) collective-permute-start(bf16[2,2,64,128]{3,2,1,0:T(8,128)(2,1)S(1)} %get-tuple-element.60), channel_id=1, source_target_pairs={{0,4},{4,8},{8,12},{12,16},{16,20},{20,24},{24,28},{1,5},{5,9},{9,... | collective-permute-start | bytes 196616 | tf_op jit(solution)/shard_map/ppermute | solution.py:15
  15.0 3.0 %copy-start.4 = (s32[2,2,3]{2,1,0:T(2,128)S(1)}, s32[2,2,3]{2,1,0:T(2,128)}, u32[]{:S(2)}) copy-start(s32[2,2,3]{2,1,0:T(2,128)} %param.14) | copy-start | bytes 148
  15.0 45.0 %collective-permute-start.2 = (bf16[2,2,128,128]{3,2,1,0:T(8,128)(2,1)S(1)}, bf16[2,2,128,128]{3,2,1,0:T(8,128)(2,1)S(1)}, u32[]{:S(2)}, u32[]{:S(2)}) collective-permute-start(bf16[2,2,128,128]{3,2,1,0:T(8,128)(2,1)S(1)} %pad_maximum_fusion.7), channel_id=1, source_target_pairs={{0,4},{4,0},{8,12},{12,8},{16,20},{20,16},{24,28},{28,24},{1,5},{5... | collective-permute-start | bytes 393224 | tf_op jit(solution)/shard_map/ppermute | solution.py:24
  18.0 0.7 copy-start.5
  58.0 0.7 slice-start
  60.2 6.4 %collective-permute-start.7 = (bf16[2,2,128,128]{3,2,1,0:T(8,128)(2,1)S(1)}, bf16[2,2,128,128]{3,2,1,0:T(8,128)(2,1)S(1)}, u32[]{:S(2)}, u32[]{:S(2)}) collective-permute-start(bf16[2,2,128,128]{3,2,1,0:T(8,128)(2,1)S(1)} %get-tuple-element.53), channel_id=1, source_target_pairs={{0,8},{4,12},{8,0},{12,4},{16,24},{20,28},{24,16},{28,20},{1,9},{5... | collective-permute-start | bytes 393224 | tf_op jit(solution)/shard_map/ppermute | solution.py:24
  60.4 9.2 %collective-permute-start.5 = (bf16[2,2,128,128]{3,2,1,0:T(8,128)(2,1)S(1)}, bf16[2,2,128,128]{3,2,1,0:T(8,128)(2,1)S(1)}, u32[]{:S(2)}, u32[]{:S(2)}) collective-permute-start(bf16[2,2,128,128]{3,2,1,0:T(8,128)(2,1)S(1)} %get-tuple-element.54), channel_id=1, source_target_pairs={{0,8},{4,12},{8,0},{12,4},{16,24},{20,28},{24,16},{28,20},{1,9},{5... | collective-permute-start | bytes 393224 | tf_op jit(solution)/shard_map/ppermute | solution.py:24
  62.5 8.6 %collective-permute-start.3 = (bf16[2,2,128,128]{3,2,1,0:T(8,128)(2,1)S(1)}, bf16[2,2,128,128]{3,2,1,0:T(8,128)(2,1)S(1)}, u32[]{:S(2)}, u32[]{:S(2)}) collective-permute-start(bf16[2,2,128,128]{3,2,1,0:T(8,128)(2,1)S(1)} %get-tuple-element.52), channel_id=1, source_target_pairs={{0,8},{4,12},{8,0},{12,4},{16,24},{20,28},{24,16},{28,20},{1,9},{5... | collective-permute-start | bytes 393224 | tf_op jit(solution)/shard_map/ppermute | solution.py:24
  66.7 9.6 %collective-permute-start.8 = (bf16[2,2,128,128]{3,2,1,0:T(8,128)(2,1)S(1)}, bf16[2,2,128,128]{3,2,1,0:T(8,128)(2,1)S(1)}, u32[]{:S(2)}, u32[]{:S(2)}) collective-permute-start(bf16[2,2,128,128]{3,2,1,0:T(8,128)(2,1)S(1)} %broadcast_select_fusion.3), channel_id=1, source_target_pairs={{0,16},{4,20},{8,24},{12,28},{16,0},{20,4},{24,8},{28,12},{1,17},{... | collective-permute-start | bytes 393224 | tf_op jit(solution)/shard_map/ppermute | solution.py:24
  69.7 8.4 %collective-permute-start.6 = (bf16[2,2,128,128]{3,2,1,0:T(8,128)(2,1)S(1)}, bf16[2,2,128,128]{3,2,1,0:T(8,128)(2,1)S(1)}, u32[]{:S(2)}, u32[]{:S(2)}) collective-permute-start(bf16[2,2,128,128]{3,2,1,0:T(8,128)(2,1)S(1)} %broadcast_select_fusion.8), channel_id=1, source_target_pairs={{0,16},{4,20},{8,24},{12,28},{16,0},{20,4},{24,8},{28,12},{1,17},{... | collective-permute-start | bytes 393224 | tf_op jit(solution)/shard_map/ppermute | solution.py:24
  71.2 8.6 %collective-permute-start.4 = (bf16[2,2,128,128]{3,2,1,0:T(8,128)(2,1)S(1)}, bf16[2,2,128,128]{3,2,1,0:T(8,128)(2,1)S(1)}, u32[]{:S(2)}, u32[]{:S(2)}) collective-permute-start(bf16[2,2,128,128]{3,2,1,0:T(8,128)(2,1)S(1)} %broadcast_select_fusion.13), channel_id=1, source_target_pairs={{0,16},{4,20},{8,24},{12,28},{16,0},{20,4},{24,8},{28,12},{1,17},{... | collective-permute-start | bytes 393224 | tf_op jit(solution)/shard_map/ppermute | solution.py:24
  82.4 0.8 copy-start.3
  86.1 11.6 %collective-permute-start.10 = (bf16[2,2,64,128]{3,2,1,0:T(8,128)(2,1)S(1)}, bf16[2,2,64,128]{3,2,1,0:T(8,128)(2,1)S(1)}, u32[]{:S(2)}, u32[]{:S(2)}) collective-permute-start(bf16[2,2,64,128]{3,2,1,0:T(8,128)(2,1)S(1)} %get-tuple-element.51), channel_id=1, source_target_pairs={{4,0},{8,4},{12,8},{16,12},{20,16},{24,20},{28,24},{5,1},{9,5},{13... | collective-permute-start | bytes 196616 | tf_op jit(solution)/shard_map/ppermute | solution.py:16
  87.4 10.3 %collective-permute-start.9 = (bf16[2,2,64,128]{3,2,1,0:T(8,128)(2,1)S(1)}, bf16[2,2,64,128]{3,2,1,0:T(8,128)(2,1)S(1)}, u32[]{:S(2)}, u32[]{:S(2)}) collective-permute-start(bf16[2,2,64,128]{3,2,1,0:T(8,128)(2,1)S(1)} %get-tuple-element.50), channel_id=1, source_target_pairs={{0,4},{4,8},{8,12},{12,16},{16,20},{20,24},{24,28},{1,5},{5,9},{9,... | collective-permute-start | bytes 196616 | tf_op jit(solution)/shard_map/ppermute | solution.py:15
  95.4 5.4 %collective-permute-start.17 = (bf16[2,2,128,128]{3,2,1,0:T(8,128)(2,1)S(1)}, bf16[2,2,128,128]{3,2,1,0:T(8,128)(2,1)S(1)}, u32[]{:S(2)}, u32[]{:S(2)}) collective-permute-start(bf16[2,2,128,128]{3,2,1,0:T(8,128)(2,1)S(1)} %bitcast.127), channel_id=1, source_target_pairs={{0,4},{4,0},{8,12},{12,8},{16,20},{20,16},{24,28},{28,24},{1,5},{5... | collective-permute-start | bytes 393224 | tf_op jit(solution)/shard_map/ppermute | solution.py:24
  95.5 6.3 %collective-permute-start.14 = (bf16[2,2,128,128]{3,2,1,0:T(8,128)(2,1)S(1)}, bf16[2,2,128,128]{3,2,1,0:T(8,128)(2,1)S(1)}, u32[]{:S(2)}, u32[]{:S(2)}) collective-permute-start(bf16[2,2,128,128]{3,2,1,0:T(8,128)(2,1)S(1)} %bitcast.125), channel_id=1, source_target_pairs={{0,4},{4,0},{8,12},{12,8},{16,20},{20,16},{24,28},{28,24},{1,5},{5... | collective-permute-start | bytes 393224 | tf_op jit(solution)/shard_map/ppermute | solution.py:24
  97.6 5.6 %collective-permute-start.11 = (bf16[2,2,128,128]{3,2,1,0:T(8,128)(2,1)S(1)}, bf16[2,2,128,128]{3,2,1,0:T(8,128)(2,1)S(1)}, u32[]{:S(2)}, u32[]{:S(2)}) collective-permute-start(bf16[2,2,128,128]{3,2,1,0:T(8,128)(2,1)S(1)} %bitcast.123), channel_id=1, source_target_pairs={{0,4},{4,0},{8,12},{12,8},{16,20},{20,16},{24,28},{28,24},{1,5},{5... | collective-permute-start | bytes 393224 | tf_op jit(solution)/shard_map/ppermute | solution.py:24
  100.9 7.5 %collective-permute-start.18 = (bf16[2,2,128,128]{3,2,1,0:T(8,128)(2,1)S(1)}, bf16[2,2,128,128]{3,2,1,0:T(8,128)(2,1)S(1)}, u32[]{:S(2)}, u32[]{:S(2)}) collective-permute-start(bf16[2,2,128,128]{3,2,1,0:T(8,128)(2,1)S(1)} %broadcast_select_fusion), channel_id=1, source_target_pairs={{0,8},{4,12},{8,0},{12,4},{16,24},{20,28},{24,16},{28,20},{1,9},{5... | collective-permute-start | bytes 393224 | tf_op jit(solution)/shard_map/ppermute | solution.py:24
  101.9 8.0 %collective-permute-start.15 = (bf16[2,2,128,128]{3,2,1,0:T(8,128)(2,1)S(1)}, bf16[2,2,128,128]{3,2,1,0:T(8,128)(2,1)S(1)}, u32[]{:S(2)}, u32[]{:S(2)}) collective-permute-start(bf16[2,2,128,128]{3,2,1,0:T(8,128)(2,1)S(1)} %broadcast_select_fusion.5), channel_id=1, source_target_pairs={{0,8},{4,12},{8,0},{12,4},{16,24},{20,28},{24,16},{28,20},{1,9},{5... | collective-permute-start | bytes 393224 | tf_op jit(solution)/shard_map/ppermute | solution.py:24
  103.3 8.2 %collective-permute-start.12 = (bf16[2,2,128,128]{3,2,1,0:T(8,128)(2,1)S(1)}, bf16[2,2,128,128]{3,2,1,0:T(8,128)(2,1)S(1)}, u32[]{:S(2)}, u32[]{:S(2)}) collective-permute-start(bf16[2,2,128,128]{3,2,1,0:T(8,128)(2,1)S(1)} %broadcast_select_fusion.10), channel_id=1, source_target_pairs={{0,8},{4,12},{8,0},{12,4},{16,24},{20,28},{24,16},{28,20},{1,9},{5... | collective-permute-start | bytes 393224 | tf_op jit(solution)/shard_map/ppermute | solution.py:24
  108.4 9.2 %collective-permute-start.19 = (bf16[2,2,128,128]{3,2,1,0:T(8,128)(2,1)S(1)}, bf16[2,2,128,128]{3,2,1,0:T(8,128)(2,1)S(1)}, u32[]{:S(2)}, u32[]{:S(2)}) collective-permute-start(bf16[2,2,128,128]{3,2,1,0:T(8,128)(2,1)S(1)} %broadcast_select_fusion.2), channel_id=1, source_target_pairs={{0,16},{4,20},{8,24},{12,28},{16,0},{20,4},{24,8},{28,12},{1,17},{... | collective-permute-start | bytes 393224 | tf_op jit(solution)/shard_map/ppermute | solution.py:24
  110.0 9.3 %collective-permute-start.16 = (bf16[2,2,128,128]{3,2,1,0:T(8,128)(2,1)S(1)}, bf16[2,2,128,128]{3,2,1,0:T(8,128)(2,1)S(1)}, u32[]{:S(2)}, u32[]{:S(2)}) collective-permute-start(bf16[2,2,128,128]{3,2,1,0:T(8,128)(2,1)S(1)} %broadcast_select_fusion.7), channel_id=1, source_target_pairs={{0,16},{4,20},{8,24},{12,28},{16,0},{20,4},{24,8},{28,12},{1,17},{... | collective-permute-start | bytes 393224 | tf_op jit(solution)/shard_map/ppermute | solution.py:24
  111.7 9.1 %collective-permute-start.13 = (bf16[2,2,128,128]{3,2,1,0:T(8,128)(2,1)S(1)}, bf16[2,2,128,128]{3,2,1,0:T(8,128)(2,1)S(1)}, u32[]{:S(2)}, u32[]{:S(2)}) collective-permute-start(bf16[2,2,128,128]{3,2,1,0:T(8,128)(2,1)S(1)} %broadcast_select_fusion.12), channel_id=1, source_target_pairs={{0,16},{4,20},{8,24},{12,28},{16,0},{20,4},{24,8},{28,12},{1,17},{... | collective-permute-start | bytes 393224 | tf_op jit(solution)/shard_map/ppermute | solution.py:24
Sparse Core Ops, SparseCore 0:
  93.2 70.8 all-reduce.5
where the time goes:
time: 175 us; the launch traced here: 174 us
  waiting for transfers between devices  71.9 us (41%)
  blocking collectives  38.6 us (22%)
  starting transfers between devices  27.4 us (16%)
  between operations  14.6 us (8%)
  local copies, waits for them, and re-layouts  10.8 us (6%)
  matrix products  7.31 us (4%)
  other arithmetic  3.48 us (2%)
    psum x1, waiting for transfers between devices, on_device(): global_total = lax.psum(global_part, 'seq')  43.2 us
    psum x1, blocking collectives, on_device(): global_sum = lax.psum(picked * owned[None, None, :, None, None], 'seq')  38.6 us
    ppermute x16, waiting for transfers between devices, swapped(): return lax.ppermute(value, axis, pairs)  28.7 us
    ppermute x16, starting transfers between devices, swapped(): return lax.ppermute(value, axis, pairs)  14.5 us
    ppermute x2, starting transfers between devices, with_halo(): before = lax.ppermute(last, axis, up)  10.3 us
  transfers between devices with their start and end apart: 21, of which 14 were waited for; matrix products, arithmetic and copies ran while one was open for 6% of the time, Pallas kernels for 0%

commit v1 on v0

--- a/solution.py
+++ b/solution.py
@@ -139,7 +139,7 @@
         rim_back[:, :, 3 * block_rows : 4 * block_rows]
     )
     global_part = jnp.sum(grads[:, :, :, 3 : 3 + global_count], axis=2)
-    global_total = lax.psum(global_part, "seq")
+    global_total = jnp.sum(lax.all_gather(global_part, "seq"), axis=0)
     global_onehot = (
         (global_local[:, None] == block_range[None, :]) & (global_owner == device)[:, None]
     ).astype(jnp.float32)

time: 175 us -> 154 us (0.88)
  waiting for transfers between devices: 71.9 us -> 50.1 us
  other arithmetic: 3.48 us -> 9.88 us
  starting transfers between devices: 27.4 us -> 24.9 us
  local copies, waits for them, and re-layouts: 10.8 us -> 8.73 us
    psum x1 -> x0, waiting for transfers between devices: 43.2 us -> none  [on_device(): global_total = lax.psum(global_part, 'seq')]
    ppermute x16, waiting for transfers between devices: 28.7 us -> 45.1 us  [swapped(): return lax.ppermute(value, axis, pairs)]
    all_gather x0 -> x1, waiting for transfers between devices: none -> 4.92 us  [on_device(): global_total = jnp.sum(lax.all_gather(global_part, 'seq'), axis=0)]
    ppermute x16, starting transfers between devices: 14.5 us -> 11.9 us  [swapped(): return lax.ppermute(value, axis, pairs)]
  transfers between devices with their start and end apart: 21 -> 21, of which waited for: 14 -> 14; matrix products, arithmetic and copies ran while one was open for 6% -> 10% of each run, Pallas kernels for 0% -> 0%
where the time goes in v1:
time: 154 us; the launch traced here: 153 us
  waiting for transfers between devices  50.1 us (33%)
  blocking collectives  38.6 us (25%)
  starting transfers between devices  24.9 us (16%)
  between operations  14.6 us (9%)
  other arithmetic  9.88 us (6%)
  local copies, waits for them, and re-layouts  8.73 us (6%)
  matrix products  6.42 us (4%)
    ppermute x16, waiting for transfers between devices, swapped(): return lax.ppermute(value, axis, pairs)  45.1 us
    psum x1, blocking collectives, on_device(): global_sum = lax.psum(picked * owned[None, None, :, None, None], 'seq')  38.6 us
    ppermute x16, starting transfers between devices, swapped(): return lax.ppermute(value, axis, pairs)  11.9 us
    ppermute x2, starting transfers between devices, with_halo(): before = lax.ppermute(last, axis, up)  10.3 us
    all_gather x1, waiting for transfers between devices, on_device(): global_total = jnp.sum(lax.all_gather(global_part, 'seq'), axis=0)  4.92 us
  transfers between devices with their start and end apart: 21, of which 14 were waited for; matrix products, arithmetic and copies ran while one was open for 10% of the time, Pallas kernels for 0%

profile of v1, /device:TPU:0, one launch (start us, length us, event | category | flops | bytes accessed | tf_op | source)
XLA Modules:
  0.0 153.2 jit_solution(9887296763784880503)
XLA Ops:
  7.2 0.9 fusion.25
  8.1 1.3 collective-permute-start.1
  9.4 5.5 %collective-permute-start = (bf16[2,2,64,128]{3,2,1,0:T(8,128)(2,1)S(1)}, bf16[2,2,64,128]{3,2,1,0:T(8,128)(2,1)S(1)}, u32[]{:S(2)}, u32[]{:S(2)}) collective-permute-start(bf16[2,2,64,128]{3,2,1,0:T(8,128)(2,1)S(1)} %get-tuple-element.60), channel_id=1, source_target_pairs={{0,4},{4,8},{8,12},{12,16},{16,20},{20,24},{24,28},{1,5},{5,9},{9,... | collective-permute-start | bytes 196616 | tf_op jit(solution)/shard_map/ppermute | solution.py:15
  14.9 0.9 pad_maximum_fusion.7
  15.8 3.0 %collective-permute-start.2 = (bf16[2,2,128,128]{3,2,1,0:T(8,128)(2,1)S(1)}, bf16[2,2,128,128]{3,2,1,0:T(8,128)(2,1)S(1)}, u32[]{:S(2)}, u32[]{:S(2)}) collective-permute-start(bf16[2,2,128,128]{3,2,1,0:T(8,128)(2,1)S(1)} %pad_maximum_fusion.7), channel_id=1, source_target_pairs={{0,4},{4,0},{8,12},{12,8},{16,20},{20,16},{24,28},{28,24},{1,5},{5... | collective-permute-start | bytes 393224 | tf_op jit(solution)/shard_map/ppermute | solution.py:24
  18.8 0.7 slice.172
  19.5 0.7 and_select_fusion
  20.2 0.7 compare_and_fusion
  20.9 0.9 pad_maximum_fusion.8
  21.8 0.6 gather_fusion
  22.5 38.6 %all-reduce.4 = bf16[2,2,2,64,128]{4,3,1,0,2:T(8,128)(2,1)S(1)} all-reduce(f32[2,2,2,64,128]{4,3,1,0,2:T(8,128)S(1)} %multiply_bitcast_fusion), channel_id=1, replica_groups=mesh['seq'=8,'head'=4] {'seq'}, use_global_device_ids=true, to_apply=%region_0.1 | all-reduce | flops 65536 | bytes 393216 | tf_op jit(solution)/shard_map/psum | solution.py:58
  61.1 0.1 copy.78
  61.6 0.3 compare_reduce_fusion.8
  61.9 0.9 pad_maximum_fusion.6
  62.8 0.1 fusion.24
  63.0 0.1 fusion.23
  63.1 0.1 fusion.22
  63.3 0.1 broadcast_select_fusion.11
  63.5 0.2 broadcast_dynamic-update-slice_fusion
  63.7 2.1 %collective-permute-start.5 = (bf16[2,2,128,128]{3,2,1,0:T(8,128)(2,1)S(1)}, bf16[2,2,128,128]{3,2,1,0:T(8,128)(2,1)S(1)}, u32[]{:S(2)}, u32[]{:S(2)}) collective-permute-start(bf16[2,2,128,128]{3,2,1,0:T(8,128)(2,1)S(1)} %get-tuple-element.54), channel_id=1, source_target_pairs={{0,8},{4,12},{8,0},{12,4},{16,24},{20,28},{24,16},{28,20},{1,9},{5... | collective-permute-start | bytes 393224 | tf_op jit(solution)/shard_map/ppermute | solution.py:24
  65.9 4.0 %collective-permute-done.7 = bf16[2,2,128,128]{3,2,1,0:T(8,128)(2,1)S(1)} collective-permute-done((bf16[2,2,128,128]{3,2,1,0:T(8,128)(2,1)S(1)}, bf16[2,2,128,128]{3,2,1,0:T(8,128)(2,1)S(1)}, u32[]{:S(2)}, u32[]{:S(2)}) %collective-permute-start.7) | collective-permute-done | bytes 131104 | tf_op jit(solution)/shard_map/ppermute | solution.py:24
  70.0 2.9 %collective-permute-done.5 = bf16[2,2,128,128]{3,2,1,0:T(8,128)(2,1)S(1)} collective-permute-done((bf16[2,2,128,128]{3,2,1,0:T(8,128)(2,1)S(1)}, bf16[2,2,128,128]{3,2,1,0:T(8,128)(2,1)S(1)}, u32[]{:S(2)}, u32[]{:S(2)}) %collective-permute-start.5) | collective-permute-done | bytes 131104 | tf_op jit(solution)/shard_map/ppermute | solution.py:24
  73.1 1.2 collective-permute-done.3
  74.4 1.7 %collective-permute-start.4 = (bf16[2,2,128,128]{3,2,1,0:T(8,128)(2,1)S(1)}, bf16[2,2,128,128]{3,2,1,0:T(8,128)(2,1)S(1)}, u32[]{:S(2)}, u32[]{:S(2)}) collective-permute-start(bf16[2,2,128,128]{3,2,1,0:T(8,128)(2,1)S(1)} %broadcast_select_fusion.13), channel_id=1, source_target_pairs={{0,16},{4,20},{8,24},{12,28},{16,0},{20,4},{24,8},{28,12},{1,17},{... | collective-permute-start | bytes 393224 | tf_op jit(solution)/shard_map/ppermute | solution.py:24
  76.2 3.5 %collective-permute-done.8 = bf16[2,2,128,128]{3,2,1,0:T(8,128)(2,1)S(1)} collective-permute-done((bf16[2,2,128,128]{3,2,1,0:T(8,128)(2,1)S(1)}, bf16[2,2,128,128]{3,2,1,0:T(8,128)(2,1)S(1)}, u32[]{:S(2)}, u32[]{:S(2)}) %collective-permute-start.8) | collective-permute-done | bytes 131104 | tf_op jit(solution)/shard_map/ppermute | solution.py:24
  79.7 0.1 copy.77
  79.9 1.8 %collective-permute-done.6 = bf16[2,2,128,128]{3,2,1,0:T(8,128)(2,1)S(1)} collective-permute-done((bf16[2,2,128,128]{3,2,1,0:T(8,128)(2,1)S(1)}, bf16[2,2,128,128]{3,2,1,0:T(8,128)(2,1)S(1)}, u32[]{:S(2)}, u32[]{:S(2)}) %collective-permute-start.6) | collective-permute-done | bytes 131104 | tf_op jit(solution)/shard_map/ppermute | solution.py:24
  81.7 0.1 copy.76
  81.9 1.2 collective-permute-done.4
  83.1 0.1 copy.75
  83.3 0.8 fusion.4
  84.1 1.2 fusion.50
  85.3 0.4 select_reduce_fusion.1
  85.7 0.2 select_reduce_fusion
  86.0 0.5 fusion.29
  86.5 0.4 fusion.9
  86.9 0.3 fusion.1
  87.2 0.4 convolution_multiply_fusion
  87.7 0.7 maximum_reduce_fusion
  88.6 1.4 collective-permute-start.10
  90.1 4.7 %collective-permute-start.9 = (bf16[2,2,64,128]{3,2,1,0:T(8,128)(2,1)S(1)}, bf16[2,2,64,128]{3,2,1,0:T(8,128)(2,1)S(1)}, u32[]{:S(2)}, u32[]{:S(2)}) collective-permute-start(bf16[2,2,64,128]{3,2,1,0:T(8,128)(2,1)S(1)} %get-tuple-element.50), channel_id=1, source_target_pairs={{0,4},{4,8},{8,12},{12,16},{16,20},{20,24},{24,28},{1,5},{5,9},{9,... | collective-permute-start | bytes 196616 | tf_op jit(solution)/shard_map/ppermute | solution.py:15
  94.9 0.9 fusion.8
  95.7 1.9 %fusion.2 = bf16[3,2,2,2,64,128]{5,3,4,1,2,0:T(2,128)(2,1)S(1)} fusion(f32[2,2,2,3,64,128]{5,4,3,2,1,0:T(8,128)S(1)} %pad_maximum_fusion, s32[2,2,3]{1,0,2:T(2,128)S(1)} %copy.78), kind=kOutput, calls=%fused_computation.8 | convolution fusion | flops 4915224 | bytes 1179696 | tf_op jit(solution)/shard_map/hqjl,chqjbd->jchlbd/dot_general | solution.py:151
  97.7 0.3 fusion.51
  98.2 2.1 %collective-permute-start.14 = (bf16[2,2,128,128]{3,2,1,0:T(8,128)(2,1)S(1)}, bf16[2,2,128,128]{3,2,1,0:T(8,128)(2,1)S(1)}, u32[]{:S(2)}, u32[]{:S(2)}) collective-permute-start(bf16[2,2,128,128]{3,2,1,0:T(8,128)(2,1)S(1)} %bitcast.126), channel_id=1, source_target_pairs={{0,4},{4,0},{8,12},{12,8},{16,20},{20,16},{24,28},{28,24},{1,5},{5... | collective-permute-start | bytes 393224 | tf_op jit(solution)/shard_map/ppermute | solution.py:24
  100.4 0.2 copy.87
  100.7 0.1 add.66
  100.8 2.6 %scatter-add.9 = f32[2,2,2,64,128]{4,2,3,1,0:T(2,128)S(1)} dynamic-update-slice(f32[2,2,2,64,128]{4,2,3,1,0:T(2,128)S(1)} %copy.87, f32[2,2,1,64,128]{4,2,3,1,0:T(1,128)S(1)} %add.66, s32[]{:T(128)} %constant.122.clone.1, s32[]{:T(128)} %constant.122.clone.1, s32[]{:T(128)} %constant.126.clone.1, s32[]{:T(128)} %constant.122.clone.1, s32[]{:T(128)} %constant.122.clone.1) | dynamic-update-slice | bytes 262148 | tf_op jit(solution)/shard_map/scatter-add | solution.py:138
  103.6 0.9 collective-permute-done.14
  104.6 1.2 collective-permute-start.15
  105.8 0.1 collective-permute-done.11
  106.0 0.8 collective-permute-start.12
  106.8 5.3 %collective-permute-done.18 = bf16[2,2,128,128]{3,2,1,0:T(8,128)(2,1)S(1)} collective-permute-done((bf16[2,2,128,128]{3,2,1,0:T(8,128)(2,1)S(1)}, bf16[2,2,128,128]{3,2,1,0:T(8,128)(2,1)S(1)}, u32[]{:S(2)}, u32[]{:S(2)}) %collective-permute-start.18) | collective-permute-done | bytes 131104 | tf_op jit(solution)/shard_map/ppermute | solution.py:24
  112.3 3.5 %collective-permute-done.15 = bf16[2,2,128,128]{3,2,1,0:T(8,128)(2,1)S(1)} collective-permute-done((bf16[2,2,128,128]{3,2,1,0:T(8,128)(2,1)S(1)}, bf16[2,2,128,128]{3,2,1,0:T(8,128)(2,1)S(1)}, u32[]{:S(2)}, u32[]{:S(2)}) %collective-permute-start.15) | collective-permute-done | bytes 131104 | tf_op jit(solution)/shard_map/ppermute | solution.py:24
  116.0 2.6 %collective-permute-done.12 = bf16[2,2,128,128]{3,2,1,0:T(8,128)(2,1)S(1)} collective-permute-done((bf16[2,2,128,128]{3,2,1,0:T(8,128)(2,1)S(1)}, bf16[2,2,128,128]{3,2,1,0:T(8,128)(2,1)S(1)}, u32[]{:S(2)}, u32[]{:S(2)}) %collective-permute-start.12) | collective-permute-done | bytes 131104 | tf_op jit(solution)/shard_map/ppermute | solution.py:24
  118.7 0.3 collective-permute-start.13
  119.1 11.3 %collective-permute-done.16 = bf16[2,2,128,128]{3,2,1,0:T(8,128)(2,1)S(1)} collective-permute-done((bf16[2,2,128,128]{3,2,1,0:T(8,128)(2,1)S(1)}, bf16[2,2,128,128]{3,2,1,0:T(8,128)(2,1)S(1)}, u32[]{:S(2)}, u32[]{:S(2)}) %collective-permute-start.16) | collective-permute-done | bytes 131104 | tf_op jit(solution)/shard_map/ppermute | solution.py:24
  130.5 6.8 %collective-permute-done.13 = bf16[2,2,128,128]{3,2,1,0:T(8,128)(2,1)S(1)} collective-permute-done((bf16[2,2,128,128]{3,2,1,0:T(8,128)(2,1)S(1)}, bf16[2,2,128,128]{3,2,1,0:T(8,128)(2,1)S(1)}, u32[]{:S(2)}, u32[]{:S(2)}) %collective-permute-start.13) | collective-permute-done | bytes 131104 | tf_op jit(solution)/shard_map/ppermute | solution.py:24
  137.4 4.9 %all-gather.3.cloned.1.call-done = f32[16,2,2,64,128]{4,3,2,1,0:T(8,128)} async-done(((f32[2,2,2,64,128]{4,3,2,1,0:T(8,128)}), f32[16,2,2,64,128]{4,3,2,1,0:T(8,128)}) %all-gather.3.cloned.1.call-update) | async-done | bytes 2097168 | tf_op jit(solution)/shard_map/all_gather | solution.py:142
  142.4 1.7 %reduce_sum.48 = f32[2,2,2,64,128]{4,3,2,1,0:T(8,128)S(1)} reduce(f32[8,2,2,2,64,128]{5,4,3,2,1,0:T(8,128)} %bitcast.107, f32[]{:T(128)} %constant.134.clone.1), dimensions={0}, to_apply=%region_5.6 | reduce | flops 458752 | bytes 2359300 | tf_op jit(solution)/shard_map/reduce_sum | solution.py:142
  144.1 0.9 fusion.7
  145.0 0.1 fusion.53
  145.1 0.6 copy.95
  145.7 0.6 copy.96
  (73 shorter events, 3.1 us)
Async XLA Ops:
  7.2 78.1 %copy-start = (bf16[2,128,128]{2,1,0:T(8,128)(2,1)S(1)}, bf16[2,128,128]{2,1,0:T(8,128)(2,1)}, u32[]{:S(2)}) copy-start(bf16[2,128,128]{2,1,0:T(8,128)(2,1)} %param.10) | copy-start | bytes 196612
  7.2 56.1 %copy-start.1 = (bf16[2,128,128]{2,1,0:T(8,128)(2,1)S(1)}, bf16[2,128,128]{2,1,0:T(8,128)(2,1)}, u32[]{:S(2)}) copy-start(bf16[2,128,128]{2,1,0:T(8,128)(2,1)} %param.11) | copy-start | bytes 196612
  7.2 56.1 %copy-start.2 = (bf16[2,128,128]{2,1,0:T(8,128)(2,1)S(1)}, bf16[2,128,128]{2,1,0:T(8,128)(2,1)}, u32[]{:S(2)}) copy-start(bf16[2,128,128]{2,1,0:T(8,128)(2,1)} %param.12) | copy-start | bytes 196612
  7.2 135.2 %all-gather.3.cloned.1.call-start = ((), (), s32[]{:S(2)}) async-start(), calls=%async_computation | async-start | bytes 2359296 | tf_op jit(solution)/shard_map/all_gather | solution.py:142
  8.1 53.7 %collective-permute-start.1 = (bf16[2,2,64,128]{3,2,1,0:T(8,128)(2,1)S(1)}, bf16[2,2,64,128]{3,2,1,0:T(8,128)(2,1)S(1)}, u32[]{:S(2)}, u32[]{:S(2)}) collective-permute-start(bf16[2,2,64,128]{3,2,1,0:T(8,128)(2,1)S(1)} %get-tuple-element.61), channel_id=1, source_target_pairs={{4,0},{8,4},{12,8},{16,12},{20,16},{24,20},{28,24},{5,1},{9,5},{13... | collective-permute-start | bytes 196616 | tf_op jit(solution)/shard_map/ppermute | solution.py:16
  9.4 52.5 %collective-permute-start = (bf16[2,2,64,128]{3,2,1,0:T(8,128)(2,1)S(1)}, bf16[2,2,64,128]{3,2,1,0:T(8,128)(2,1)S(1)}, u32[]{:S(2)}, u32[]{:S(2)}) collective-permute-start(bf16[2,2,64,128]{3,2,1,0:T(8,128)(2,1)S(1)} %get-tuple-element.60), channel_id=1, source_target_pairs={{0,4},{4,8},{8,12},{12,16},{16,20},{20,24},{24,28},{1,5},{5,9},{9,... | collective-permute-start | bytes 196616 | tf_op jit(solution)/shard_map/ppermute | solution.py:15
  15.8 47.4 %collective-permute-start.2 = (bf16[2,2,128,128]{3,2,1,0:T(8,128)(2,1)S(1)}, bf16[2,2,128,128]{3,2,1,0:T(8,128)(2,1)S(1)}, u32[]{:S(2)}, u32[]{:S(2)}) collective-permute-start(bf16[2,2,128,128]{3,2,1,0:T(8,128)(2,1)S(1)} %pad_maximum_fusion.7), channel_id=1, source_target_pairs={{0,4},{4,0},{8,12},{12,8},{16,20},{20,16},{24,28},{28,24},{1,5},{5... | collective-permute-start | bytes 393224 | tf_op jit(solution)/shard_map/ppermute | solution.py:24
  63.4 6.4 %collective-permute-start.7 = (bf16[2,2,128,128]{3,2,1,0:T(8,128)(2,1)S(1)}, bf16[2,2,128,128]{3,2,1,0:T(8,128)(2,1)S(1)}, u32[]{:S(2)}, u32[]{:S(2)}) collective-permute-start(bf16[2,2,128,128]{3,2,1,0:T(8,128)(2,1)S(1)} %get-tuple-element.53), channel_id=1, source_target_pairs={{0,8},{4,12},{8,0},{12,4},{16,24},{20,28},{24,16},{28,20},{1,9},{5... | collective-permute-start | bytes 393224 | tf_op jit(solution)/shard_map/ppermute | solution.py:24
  63.7 9.2 %collective-permute-start.5 = (bf16[2,2,128,128]{3,2,1,0:T(8,128)(2,1)S(1)}, bf16[2,2,128,128]{3,2,1,0:T(8,128)(2,1)S(1)}, u32[]{:S(2)}, u32[]{:S(2)}) collective-permute-start(bf16[2,2,128,128]{3,2,1,0:T(8,128)(2,1)S(1)} %get-tuple-element.54), channel_id=1, source_target_pairs={{0,8},{4,12},{8,0},{12,4},{16,24},{20,28},{24,16},{28,20},{1,9},{5... | collective-permute-start | bytes 393224 | tf_op jit(solution)/shard_map/ppermute | solution.py:24
  65.8 8.6 %collective-permute-start.3 = (bf16[2,2,128,128]{3,2,1,0:T(8,128)(2,1)S(1)}, bf16[2,2,128,128]{3,2,1,0:T(8,128)(2,1)S(1)}, u32[]{:S(2)}, u32[]{:S(2)}) collective-permute-start(bf16[2,2,128,128]{3,2,1,0:T(8,128)(2,1)S(1)} %get-tuple-element.52), channel_id=1, source_target_pairs={{0,8},{4,12},{8,0},{12,4},{16,24},{20,28},{24,16},{28,20},{1,9},{5... | collective-permute-start | bytes 393224 | tf_op jit(solution)/shard_map/ppermute | solution.py:24
  69.9 9.7 %collective-permute-start.8 = (bf16[2,2,128,128]{3,2,1,0:T(8,128)(2,1)S(1)}, bf16[2,2,128,128]{3,2,1,0:T(8,128)(2,1)S(1)}, u32[]{:S(2)}, u32[]{:S(2)}) collective-permute-start(bf16[2,2,128,128]{3,2,1,0:T(8,128)(2,1)S(1)} %broadcast_select_fusion.3), channel_id=1, source_target_pairs={{0,16},{4,20},{8,24},{12,28},{16,0},{20,4},{24,8},{28,12},{1,17},{... | collective-permute-start | bytes 393224 | tf_op jit(solution)/shard_map/ppermute | solution.py:24
  73.0 8.6 %collective-permute-start.6 = (bf16[2,2,128,128]{3,2,1,0:T(8,128)(2,1)S(1)}, bf16[2,2,128,128]{3,2,1,0:T(8,128)(2,1)S(1)}, u32[]{:S(2)}, u32[]{:S(2)}) collective-permute-start(bf16[2,2,128,128]{3,2,1,0:T(8,128)(2,1)S(1)} %broadcast_select_fusion.8), channel_id=1, source_target_pairs={{0,16},{4,20},{8,24},{12,28},{16,0},{20,4},{24,8},{28,12},{1,17},{... | collective-permute-start | bytes 393224 | tf_op jit(solution)/shard_map/ppermute | solution.py:24
  74.4 8.6 %collective-permute-start.4 = (bf16[2,2,128,128]{3,2,1,0:T(8,128)(2,1)S(1)}, bf16[2,2,128,128]{3,2,1,0:T(8,128)(2,1)S(1)}, u32[]{:S(2)}, u32[]{:S(2)}) collective-permute-start(bf16[2,2,128,128]{3,2,1,0:T(8,128)(2,1)S(1)} %broadcast_select_fusion.13), channel_id=1, source_target_pairs={{0,16},{4,20},{8,24},{12,28},{16,0},{20,4},{24,8},{28,12},{1,17},{... | collective-permute-start | bytes 393224 | tf_op jit(solution)/shard_map/ppermute | solution.py:24
  84.0 1.9 %copy-start.5 = (bf16[2,128,128]{2,1,0:T(8,128)(2,1)S(1)}, bf16[2,128,128]{2,1,0:T(8,128)(2,1)}, u32[]{:S(2)}) copy-start(bf16[2,128,128]{2,1,0:T(8,128)(2,1)} %param.13) | copy-start | bytes 196612
  85.3 1.6 %copy-start.3 = (bf16[1,2,2,8,64,128]{5,2,4,0,3,1:T(2,128)(2,1)}, bf16[1,2,2,8,64,128]{5,2,4,0,3,1:T(2,128)(2,1)S(1)}, u32[]{:S(2)}) copy-start(bf16[1,2,2,8,64,128]{5,2,4,0,3,1:T(2,128)(2,1)S(1)} %get-tuple-element.45) | copy-start | bytes 1572868
  88.5 6.4 %copy-start.4 = (bf16[1,2,2,8,64,128]{5,2,4,0,3,1:T(2,128)(2,1)S(1)}, bf16[1,2,2,8,64,128]{5,2,4,0,3,1:T(2,128)(2,1)}, u32[]{:S(2)}) copy-start(bf16[1,2,2,8,64,128]{5,2,4,0,3,1:T(2,128)(2,1)} %copy-done.3) | copy-start | bytes 1572868
  88.6 11.7 %collective-permute-start.10 = (bf16[2,2,64,128]{3,2,1,0:T(8,128)(2,1)S(1)}, bf16[2,2,64,128]{3,2,1,0:T(8,128)(2,1)S(1)}, u32[]{:S(2)}, u32[]{:S(2)}) collective-permute-start(bf16[2,2,64,128]{3,2,1,0:T(8,128)(2,1)S(1)} %get-tuple-element.51), channel_id=1, source_target_pairs={{4,0},{8,4},{12,8},{16,12},{20,16},{24,20},{28,24},{5,1},{9,5},{13... | collective-permute-start | bytes 196616 | tf_op jit(solution)/shard_map/ppermute | solution.py:16
  90.1 10.3 %collective-permute-start.9 = (bf16[2,2,64,128]{3,2,1,0:T(8,128)(2,1)S(1)}, bf16[2,2,64,128]{3,2,1,0:T(8,128)(2,1)S(1)}, u32[]{:S(2)}, u32[]{:S(2)}) collective-permute-start(bf16[2,2,64,128]{3,2,1,0:T(8,128)(2,1)S(1)} %get-tuple-element.50), channel_id=1, source_target_pairs={{0,4},{4,8},{8,12},{12,16},{16,20},{20,24},{24,28},{1,5},{5,9},{9,... | collective-permute-start | bytes 196616 | tf_op jit(solution)/shard_map/ppermute | solution.py:15
  98.1 5.4 %collective-permute-start.17 = (bf16[2,2,128,128]{3,2,1,0:T(8,128)(2,1)S(1)}, bf16[2,2,128,128]{3,2,1,0:T(8,128)(2,1)S(1)}, u32[]{:S(2)}, u32[]{:S(2)}) collective-permute-start(bf16[2,2,128,128]{3,2,1,0:T(8,128)(2,1)S(1)} %bitcast.128), channel_id=1, source_target_pairs={{0,4},{4,0},{8,12},{12,8},{16,20},{20,16},{24,28},{28,24},{1,5},{5... | collective-permute-start | bytes 393224 | tf_op jit(solution)/shard_map/ppermute | solution.py:24
  98.2 6.3 %collective-permute-start.14 = (bf16[2,2,128,128]{3,2,1,0:T(8,128)(2,1)S(1)}, bf16[2,2,128,128]{3,2,1,0:T(8,128)(2,1)S(1)}, u32[]{:S(2)}, u32[]{:S(2)}) collective-permute-start(bf16[2,2,128,128]{3,2,1,0:T(8,128)(2,1)S(1)} %bitcast.126), channel_id=1, source_target_pairs={{0,4},{4,0},{8,12},{12,8},{16,20},{20,16},{24,28},{28,24},{1,5},{5... | collective-permute-start | bytes 393224 | tf_op jit(solution)/shard_map/ppermute | solution.py:24
  100.3 5.6 %collective-permute-start.11 = (bf16[2,2,128,128]{3,2,1,0:T(8,128)(2,1)S(1)}, bf16[2,2,128,128]{3,2,1,0:T(8,128)(2,1)S(1)}, u32[]{:S(2)}, u32[]{:S(2)}) collective-permute-start(bf16[2,2,128,128]{3,2,1,0:T(8,128)(2,1)S(1)} %bitcast.124), channel_id=1, source_target_pairs={{0,4},{4,0},{8,12},{12,8},{16,20},{20,16},{24,28},{28,24},{1,5},{5... | collective-permute-start | bytes 393224 | tf_op jit(solution)/shard_map/ppermute | solution.py:24
  103.5 8.6 %collective-permute-start.18 = (bf16[2,2,128,128]{3,2,1,0:T(8,128)(2,1)S(1)}, bf16[2,2,128,128]{3,2,1,0:T(8,128)(2,1)S(1)}, u32[]{:S(2)}, u32[]{:S(2)}) collective-permute-start(bf16[2,2,128,128]{3,2,1,0:T(8,128)(2,1)S(1)} %broadcast_select_fusion), channel_id=1, source_target_pairs={{0,8},{4,12},{8,0},{12,4},{16,24},{20,28},{24,16},{28,20},{1,9},{5... | collective-permute-start | bytes 393224 | tf_op jit(solution)/shard_map/ppermute | solution.py:24
  104.6 11.2 %collective-permute-start.15 = (bf16[2,2,128,128]{3,2,1,0:T(8,128)(2,1)S(1)}, bf16[2,2,128,128]{3,2,1,0:T(8,128)(2,1)S(1)}, u32[]{:S(2)}, u32[]{:S(2)}) collective-permute-start(bf16[2,2,128,128]{3,2,1,0:T(8,128)(2,1)S(1)} %broadcast_select_fusion.5), channel_id=1, source_target_pairs={{0,8},{4,12},{8,0},{12,4},{16,24},{20,28},{24,16},{28,20},{1,9},{5... | collective-permute-start | bytes 393224 | tf_op jit(solution)/shard_map/ppermute | solution.py:24
  106.0 12.6 %collective-permute-start.12 = (bf16[2,2,128,128]{3,2,1,0:T(8,128)(2,1)S(1)}, bf16[2,2,128,128]{3,2,1,0:T(8,128)(2,1)S(1)}, u32[]{:S(2)}, u32[]{:S(2)}) collective-permute-start(bf16[2,2,128,128]{3,2,1,0:T(8,128)(2,1)S(1)} %broadcast_select_fusion.10), channel_id=1, source_target_pairs={{0,8},{4,12},{8,0},{12,4},{16,24},{20,28},{24,16},{28,20},{1,9},{5... | collective-permute-start | bytes 393224 | tf_op jit(solution)/shard_map/ppermute | solution.py:24
  112.2 6.8 %collective-permute-start.19 = (bf16[2,2,128,128]{3,2,1,0:T(8,128)(2,1)S(1)}, bf16[2,2,128,128]{3,2,1,0:T(8,128)(2,1)S(1)}, u32[]{:S(2)}, u32[]{:S(2)}) collective-permute-start(bf16[2,2,128,128]{3,2,1,0:T(8,128)(2,1)S(1)} %broadcast_select_fusion.2), channel_id=1, source_target_pairs={{0,16},{4,20},{8,24},{12,28},{16,0},{20,4},{24,8},{28,12},{1,17},{... | collective-permute-start | bytes 393224 | tf_op jit(solution)/shard_map/ppermute | solution.py:24
  115.9 14.5 %collective-permute-start.16 = (bf16[2,2,128,128]{3,2,1,0:T(8,128)(2,1)S(1)}, bf16[2,2,128,128]{3,2,1,0:T(8,128)(2,1)S(1)}, u32[]{:S(2)}, u32[]{:S(2)}) collective-permute-start(bf16[2,2,128,128]{3,2,1,0:T(8,128)(2,1)S(1)} %broadcast_select_fusion.7), channel_id=1, source_target_pairs={{0,16},{4,20},{8,24},{12,28},{16,0},{20,4},{24,8},{28,12},{1,17},{... | collective-permute-start | bytes 393224 | tf_op jit(solution)/shard_map/ppermute | solution.py:24
  118.7 18.6 %collective-permute-start.13 = (bf16[2,2,128,128]{3,2,1,0:T(8,128)(2,1)S(1)}, bf16[2,2,128,128]{3,2,1,0:T(8,128)(2,1)S(1)}, u32[]{:S(2)}, u32[]{:S(2)}) collective-permute-start(bf16[2,2,128,128]{3,2,1,0:T(8,128)(2,1)S(1)} %broadcast_select_fusion.12), channel_id=1, source_target_pairs={{0,16},{4,20},{8,24},{12,28},{16,0},{20,4},{24,8},{28,12},{1,17},{... | collective-permute-start | bytes 393224 | tf_op jit(solution)/shard_map/ppermute | solution.py:24
Sparse Core Ops, SparseCore 0:
  88.6 53.6 all-gather.2
